TPU v7x, 128 devices: a whole 4x4x4 slice. The times are simulated.
128 devices in a mesh: dp: 8 (over x_lo, y), expert: 16 (over x_hi, z, core).
Axes of the slice: x: 4 (x_hi: 2, x_lo: 2; x = x_hi * 2 + x_lo), y: 4, z: 4, core: 2. Of those that a mesh axis runs over, the one named last changes fastest.
Arguments:
- tokens: bfloat16 [65536, 2048], P(('dp', 'expert')), may hold values from -6 to 6
- probe: bfloat16 [65536, 2048], P(('dp', 'expert')), may hold values from -20 to 20
- domain: int32 [65536], P(('dp', 'expert')), may hold values from 0 to 21
- mix: float32 [22], replicated, may hold values from 0.5 to 2
- router: bfloat16 [2048, 32], replicated, may hold values from -0.125 to 0.125
- picks: int32 [128, 32, 40], P(('dp', 'expert')), may hold values from 0 to 511, as said below
- w_gate: bfloat16 [2048, 32, 768], P(None, 'expert'), may hold values from -0.125 to 0.125
- w_up: bfloat16 [2048, 32, 768], P(None, 'expert'), may hold values from -0.125 to 0.125
- w_down: bfloat16 [2048, 32, 768], P(None, 'expert'), may hold values from -0.21875 to 0.21875
Outputs:
- domain_loss: float32 [22], replicated
- router_grad: float32 [2048, 32], replicated
- grad_gate: bfloat16 [2048, 32, 768], P('dp', 'expert')
- grad_up: bfloat16 [2048, 32, 768], P('dp', 'expert')
- grad_down: bfloat16 [2048, 32, 768], P('dp', 'expert')
Inputs may be any that keep to these rules, and one draw needn't show every extreme that they name: The 40 picks of one expert on one device are distinct token positions of that device.
All inputs are finite; a program needn't handle non-finite values.
Results may differ from a plain program's by a relative error of at most 0.018.
Values may be sent and summed in bfloat16 or wider, within the bound.
A program may use at most 192 MiB of HBM per device.

v0:
```python
import math
import jax
import jax.numpy as jnp
from jax import lax
from jax.sharding import PartitionSpec as P

BF = jnp.bfloat16
F32 = jnp.float32


def body(tokens, probe, domain, mix, router, picks, w_gate, w_up, w_down):
    token_count, model_width = tokens.shape
    expert_count = router.shape[1]
    slot_count = picks.shape[2]
    pick_count = expert_count * slot_count
    domain_count = mix.shape[0]
    device_count = lax.axis_size("dp") * lax.axis_size("expert")
    flat = picks[0].reshape(pick_count)
    token_ids = jnp.arange(token_count, dtype=jnp.int32)
    select = (flat[:, None] == token_ids[None, :]).astype(BF)
    expert_of = jnp.repeat(jnp.arange(expert_count, dtype=jnp.int32), slot_count)
    own_expert = expert_of[:, None] == jnp.arange(expert_count, dtype=jnp.int32)[None, :]
    outgoing = jnp.dot(select, tokens, preferred_element_type=F32).astype(BF)
    received = lax.all_to_all(
        outgoing.reshape(expert_count, 1, slot_count, model_width),
        "expert",
        split_axis=0,
        concat_axis=1,
        tiled=True,
    )
    logits = jnp.dot(outgoing, router, preferred_element_type=F32)
    gate = jax.nn.sigmoid(jnp.sum(jnp.where(own_expert, logits, 0.0), axis=1))
    pre_gate = jnp.einsum("jsrd,djf->jsrf", received, w_gate, preferred_element_type=F32)
    pre_up = jnp.einsum("jsrd,djf->jsrf", received, w_up, preferred_element_type=F32)
    hidden = (jax.nn.silu(pre_gate) * pre_up).astype(BF)
    result = jnp.einsum("jsrf,djf->jsrd", hidden, w_down, preferred_element_type=F32).astype(BF)
    returned = lax.all_to_all(result, "expert", split_axis=1, concat_axis=0, tiled=True)
    returned = returned.reshape(pick_count, model_width)
    weighted = jnp.where(
        flat[None, :] == token_ids[:, None], gate.astype(BF)[None, :], jnp.zeros((), BF)
    )
    added = jnp.dot(weighted, returned, preferred_element_type=F32)
    difference = tokens.astype(F32) + added - probe.astype(F32)
    per_token = jnp.sum(difference * difference, axis=1)
    member = (domain[:, None] == jnp.arange(domain_count, dtype=jnp.int32)[None, :]).astype(F32)
    local_loss = jnp.sum(per_token[:, None] * member, axis=0)
    loss_scale = 1.0 / math.sqrt(device_count * slot_count)
    weight_tok = jnp.sum(member * mix[None, :], axis=1)
    upstream = ((loss_scale * weight_tok)[:, None] * difference).astype(BF)
    picked_up = jnp.dot(select, upstream, preferred_element_type=F32)
    sending = (gate[:, None] * picked_up).astype(BF)
    gate_slope = jnp.sum(picked_up * returned.astype(F32), axis=1)
    logit_grad = gate_slope * gate * (1.0 - gate)
    placing = jnp.where(own_expert, logit_grad[:, None], 0.0)
    high = placing.astype(BF)
    low = (placing - high.astype(F32)).astype(BF)
    placed = lax.dot_general(
        select,
        jnp.concatenate([high, low], axis=1),
        (((0,), (0,)), ((), ())),
        preferred_element_type=F32,
    ).astype(BF)
    router_part = lax.dot_general(
        tokens, placed, (((0,), (0,)), ((), ())), preferred_element_type=F32
    )
    router_part = router_part[:, :expert_count] + router_part[:, expert_count:]
    loss_rows = jnp.zeros((8, expert_count), F32).at[0, :domain_count].set(local_loss)
    summed = lax.psum(jnp.concatenate([router_part, loss_rows], axis=0), ("dp", "expert"))
    back_grad = lax.all_to_all(
        sending.reshape(expert_count, 1, slot_count, model_width),
        "expert",
        split_axis=0,
        concat_axis=1,
        tiled=True,
    )

    def reduced(left, right):
        part = jnp.einsum("jsrd,jsrf->djf", left, right, preferred_element_type=F32)
        return lax.psum_scatter(part.astype(BF), "dp", scatter_dimension=0, tiled=True)

    grad_down = reduced(back_grad, hidden)
    hidden_grad = jnp.einsum("jsrd,djf->jsrf", back_grad, w_down, preferred_element_type=F32)
    sigmoid_gate = jax.nn.sigmoid(pre_gate)
    gate_in = (
        hidden_grad * pre_up * sigmoid_gate * (1.0 + pre_gate * (1.0 - sigmoid_gate))
    ).astype(BF)
    up_in = (hidden_grad * (pre_gate * sigmoid_gate)).astype(BF)
    grad_gate = reduced(received, gate_in)
    grad_up = reduced(received, up_in)
    domain_loss = summed[model_width, :domain_count] * (
        domain_count / (token_count * device_count * model_width)
    )
    return (domain_loss, summed[:model_width], grad_gate, grad_up, grad_down)


def solution(mesh):
    placed = (
        P(("dp", "expert"), None),
        P(("dp", "expert"), None),
        P(("dp", "expert")),
        P(),
        P(),
        P(("dp", "expert"), None, None),
        P(None, "expert", None),
        P(None, "expert", None),
        P(None, "expert", None),
    )
    return jax.shard_map(
        body,
        mesh=mesh,
        in_specs=placed,
        out_specs=(
            P(),
            P(),
            P("dp", "expert", None),
            P("dp", "expert", None),
            P("dp", "expert", None),
        ),
        check_vma=False,
    )
```

profile of v0, /device:TPU:1, one launch (start us, length us, event | category | flops | bytes accessed | tf_op | source)
XLA Modules:
  0.0 530.8 jit_solution(12913081817586084446)
XLA Ops:
  8.9 4.9 convolution_convert_fusion
  13.8 71.2 %all_to_all.51 = bf16[32,1,40,2048]{3,2,1,0:T(8,128)(2,1)S(1)} all-to-all(bf16[32,1,40,2048]{3,2,1,0:T(8,128)(2,1)S(1)} %bitcast.69), channel_id=1, replica_groups=mesh['dp'=8,'expert'=16] {'expert'}, dimensions={0} | all-to-all | bytes 10485760 | tf_op jit(solution)/shard_map/all_to_all | solution.py:24
  85.0 4.4 fusion.5
  89.4 6.5 %multiply_convert_fusion.4 = (bf16[2,16,40,768]{3,2,1,0:T(8,128)(2,1)}, f32[2,16,40,768]{3,2,1,0:T(8,128)}) fusion(f32[2,16,40,768]{3,2,1,0:T(8,128)S(1)} %fusion.5, bf16[2048,2,768,1]{2,1,0,3:T(2,128)(2,1)S(1)} %bitcast.79, bf16[16,2,1,40,2048]{4,3,1,0,2:T(8,128)(2,1)S(1)} %bitcast.71), kind=kOutput, calls=%fused_computation.31 | convolution fusion | flops 4032430080 | bytes 21364736 | tf_op jit(solution)/shard_map/jsrd,djf->jsrf/dot_general | solution.py:34
  96.0 7.7 %fusion.19 = bf16[2,16,40,2048]{3,2,1,0:T(8,128)(2,1)S(1)} fusion(bf16[2,16,40,768]{3,2,1,0:T(8,128)(2,1)} %get-tuple-element.43, bf16[2048,2,768,1]{2,1,0,3:T(2,128)(2,1)} %bitcast.80), kind=kOutput, calls=%fused_computation.28 | convolution fusion | flops 4029153280 | bytes 13500416 | tf_op jit(solution)/shard_map/jsrf,djf->jsrd/dot_general | solution.py:36
  103.6 2.8 copy.51
  106.4 5.7 %all-to-all-start.1 = ((bf16[2,16,40,2048]{3,2,0,1:T(8,128)(2,1)}), bf16[2,16,40,2048]{3,2,0,1:T(8,128)(2,1)}, u32[]{:S(2)}, u32[]{:S(2)}) async-start(bf16[2,16,40,2048]{3,2,0,1:T(8,128)(2,1)} %copy.51), calls=%async_computation.1 | async-start | bytes 10485760 | tf_op jit(solution)/shard_map/all_to_all | solution.py:37
  112.2 4.3 fusion.38
  116.6 64.9 %all-to-all-done.1 = bf16[2,16,40,2048]{3,2,0,1:T(8,128)(2,1)} async-done(((bf16[2,16,40,2048]{3,2,0,1:T(8,128)(2,1)}), bf16[2,16,40,2048]{3,2,0,1:T(8,128)(2,1)}, u32[]{:S(2)}, u32[]{:S(2)}) %all-to-all-start.1) | async-done | bytes 5242912 | tf_op jit(solution)/shard_map/all_to_all | solution.py:37
  181.5 6.5 %multiply_reduce_fusion.1 = (f32[512]{0:T(512)S(1)}, f32[512,2048]{1,0:T(8,128)S(1)}) fusion(bf16[512,2048]{1,0:T(8,128)(2,1)} %param.12, bf16[1280,2048]{1,0:T(8,128)(2,1)} %bitcast.11, s32[1280]{0:T(1024)S(1)} %eq.64, bf16[1280]{0:T(1024)(128)(2,1)S(1)} %get-tuple-element.42, bf16[512,2048]{1,0:T(8,128)(2,1)S(1)} %copy-done.4), kind=kOutput, calls=%fused_computation.25 | convolution fusion | flops 2691956224 | bytes 13641216 | tf_op jit(solution)/shard_map/dot_general | solution.py:42
  188.1 7.4 %multiply_convert_fusion = (bf16[1280,2048]{1,0:T(8,128)(2,1)}, f32[1280]{0:T(1024)S(1)}) fusion(f32[1280]{0:T(1024)S(1)} %get-tuple-element.41, bf16[2,16,40,2048]{3,2,0,1:T(8,128)(2,1)} %all-to-all-done.1, f32[512,2048]{1,0:T(8,128)S(1)} %get-tuple-element.46, f32[512]{0:T(512)S(1)} %broadcast_multiply_fusion, s32[1280]{0:T(1024)S(1)} %eq.64), kind=kOutput, calls=%fused_computation.3 | convolution fusion | flops 2700212992 | bytes 14697472 | tf_op jit(solution)/shard_map/dot_general | solution.py:50
  195.5 14.7 %all-to-all-start.2 = ((bf16[32,1,40,2048]{3,2,1,0:T(8,128)(2,1)}), bf16[32,1,40,2048]{3,2,1,0:T(8,128)(2,1)}, u32[]{:S(2)}, u32[]{:S(2)}) async-start(bf16[32,1,40,2048]{3,2,1,0:T(8,128)(2,1)} %bitcast.74), calls=%async_computation.2 | async-start | bytes 10485760 | tf_op jit(solution)/shard_map/all_to_all | solution.py:69
  212.3 68.4 %all-to-all-done.2 = bf16[32,1,40,2048]{3,2,1,0:T(8,128)(2,1)} async-done(((bf16[32,1,40,2048]{3,2,1,0:T(8,128)(2,1)}), bf16[32,1,40,2048]{3,2,1,0:T(8,128)(2,1)}, u32[]{:S(2)}, u32[]{:S(2)}) %all-to-all-start.2) | async-done | bytes 5242912 | tf_op jit(solution)/shard_map/all_to_all | solution.py:69
  280.7 9.8 %fusion.2 = bf16[2048,2,768]{0,2,1:T(8,128)(2,1)} fusion(bf16[2,16,40,768]{3,2,1,0:T(8,128)(2,1)} %get-tuple-element.43, bf16[16,2,1,40,2048]{4,3,1,0,2:T(8,128)(2,1)} %bitcast.18), kind=kOutput, calls=%fused_computation.8 | convolution fusion | flops 4029677568 | bytes 13500416 | tf_op jit(solution)/shard_map/jsrd,jsrf->djf/dot_general | solution.py:78
  290.8 8.2 %fusion.7 = f32[2,16,40,768]{3,2,1,0:T(8,128)S(1)} fusion(bf16[2048,2,768,1]{2,1,0,3:T(2,128)(2,1)} %bitcast.81, bf16[16,2,1,40,2048]{4,3,1,0,2:T(8,128)(2,1)} %bitcast.18), kind=kOutput, calls=%fused_computation.13 | convolution fusion | flops 4026531840 | bytes 15466496 | tf_op jit(solution)/shard_map/jsrd,djf->jsrf/dot_general | solution.py:82
  299.0 1.8 copy-done.10
  300.9 9.9 %fusion.1 = bf16[2048,2,768]{0,2,1:T(8,128)(2,1)} fusion(bf16[16,2,1,40,2048]{4,3,1,0,2:T(8,128)(2,1)} %bitcast.72, f32[2,16,40,768]{3,2,1,0:T(8,128)S(1)} %fusion.7, f32[2,16,40,768]{3,2,1,0:T(8,128)S(1)} %copy-done.9), kind=kOutput, calls=%fused_computation.7 | convolution fusion | flops 4035575808 | bytes 19398656 | tf_op jit(solution)/shard_map/jsrd,jsrf->djf/dot_general | solution.py:78
  310.8 12.3 %fusion = bf16[2048,2,768]{0,2,1:T(8,128)(2,1)} fusion(bf16[16,2,1,40,2048]{4,3,1,0,2:T(8,128)(2,1)} %bitcast.73, f32[2,16,40,768]{3,2,1,0:T(8,128)} %copy-done.8, f32[2,16,40,768]{3,2,1,0:T(8,128)} %copy-done.10, f32[2,16,40,768]{3,2,1,0:T(8,128)} %get-tuple-element.44), kind=kOutput, calls=%fused_computation.6 | convolution fusion | flops 4039507968 | bytes 23330816 | tf_op jit(solution)/shard_map/jsrd,jsrf->djf/dot_general | solution.py:78
  323.2 129.6 %all-reduce.3.cloned.1.call-done = f32[2056,32]{0,1:T(8,128)} async-done(((f32[2056,32]{0,1:T(8,128)}), f32[2056,32]{0,1:T(8,128)}) %all-reduce.3.cloned.1.call-update) | async-done | bytes 263184 | tf_op jit(solution)/shard_map/psum | solution.py:68
  452.8 1.7 slice.35
  455.8 3.1 copy.58
  458.9 3.0 copy.57
  461.9 58.3 %reduce-scatter.4.cloned.1.call-done = bf16[256,2,768]{0,2,1:T(8,128)(2,1)} async-done(((bf16[2048,2,768]{0,2,1:T(8,128)(2,1)}), bf16[256,2,768]{0,2,1:T(8,128)(2,1)}) %reduce-scatter.4.cloned.1.call-update) | async-done | bytes 786448 | tf_op jit(solution)/shard_map/reduce_scatter | solution.py:79
  520.2 3.0 copy.56
  (50 shorter events, 4.9 us)
Async XLA Ops:
  8.0 104.2 %copy-start = (bf16[2048,32]{0,1:T(8,128)(2,1)S(1)}, bf16[2048,32]{0,1:T(8,128)(2,1)}, u32[]{:S(2)}) copy-start(bf16[2048,32]{0,1:T(8,128)(2,1)} %param.15) | copy-start | bytes 393220
  13.8 71.2 %copy-start.2 = (bf16[1280,2048]{1,0:T(8,128)(2,1)}, bf16[1280,2048]{1,0:T(8,128)(2,1)S(1)}, u32[]{:S(2)}) copy-start(bf16[1280,2048]{1,0:T(8,128)(2,1)S(1)} %convolution_convert_fusion) | copy-start | bytes 15728644
  13.8 71.2 %copy-start.7 = (bf16[2048,2,768]{2,1,0:T(2,128)(2,1)S(1)}, bf16[2048,2,768]{2,1,0:T(2,128)(2,1)}, u32[]{:S(2)}) copy-start(bf16[2048,2,768]{2,1,0:T(2,128)(2,1)} %param.17) | copy-start | bytes 18874372
  13.8 75.6 %slice-start = ((s8[6291456]{0:T(1024)(128)(4,1)}), s8[4194304]{0:T(1024)(128)(4,1)S(1)}, s32[]{:S(2)}) async-start(s8[6291456]{0:T(1024)(128)(4,1)} %bitcast.77), calls=%async_computation.10 | async-start | bytes 8388608
  85.0 4.4 copy-start.3
  85.0 4.4 slice-start.1
  89.4 6.6 %copy-start.8 = (f32[2,16,40,768]{3,2,1,0:T(8,128)}, f32[2,16,40,768]{3,2,1,0:T(8,128)S(1)}, u32[]{:S(2)}) copy-start(f32[2,16,40,768]{3,2,1,0:T(8,128)S(1)} %fusion.5) | copy-start | bytes 11796484
  106.4 75.0 %all-to-all-start.1 = ((bf16[2,16,40,2048]{3,2,0,1:T(8,128)(2,1)}), bf16[2,16,40,2048]{3,2,0,1:T(8,128)(2,1)}, u32[]{:S(2)}, u32[]{:S(2)}) async-start(bf16[2,16,40,2048]{3,2,0,1:T(8,128)(2,1)} %copy.51), calls=%async_computation.1 | async-start | bytes 10485760 | tf_op jit(solution)/shard_map/all_to_all | solution.py:37
  112.1 69.3 %copy-start.4 = (bf16[512,2048]{1,0:T(8,128)(2,1)S(1)}, bf16[512,2048]{1,0:T(8,128)(2,1)}, u32[]{:S(2)}) copy-start(bf16[512,2048]{1,0:T(8,128)(2,1)} %param.11) | copy-start | bytes 6291460
  181.5 6.5 %copy-start.5 = (s32[512]{0:T(512)S(1)}, s32[512]{0:T(512)}, u32[]{:S(2)}) copy-start(s32[512]{0:T(512)} %param.13) | copy-start | bytes 6148
  181.5 6.5 %copy-start.6 = (f32[22]{0:T(128)S(1)}, f32[22]{0:T(128)}, u32[]{:S(2)}) copy-start(f32[22]{0:T(128)} %param.14) | copy-start | bytes 268
  195.5 85.2 %all-to-all-start.2 = ((bf16[32,1,40,2048]{3,2,1,0:T(8,128)(2,1)}), bf16[32,1,40,2048]{3,2,1,0:T(8,128)(2,1)}, u32[]{:S(2)}, u32[]{:S(2)}) async-start(bf16[32,1,40,2048]{3,2,1,0:T(8,128)(2,1)} %bitcast.74), calls=%async_computation.2 | async-start | bytes 10485760 | tf_op jit(solution)/shard_map/all_to_all | solution.py:69
  210.2 242.6 %all-reduce.3.cloned.1.call-start = ((), (), s32[]{:S(2)}) async-start(), calls=%async_computation.6 | async-start | bytes 557056 | tf_op jit(solution)/shard_map/psum | solution.py:68
  212.2 243.5 %reduce-scatter.8.cloned.1.call-start = ((), (), s32[]{:S(2)}) async-start(), calls=%async_computation.9 | async-start | bytes 7077888 | tf_op jit(solution)/shard_map/reduce_scatter | solution.py:79
  290.5 168.3 %reduce-scatter.6.cloned.1.call-start = ((), (), s32[]{:S(2)}) async-start(), calls=%async_computation.8 | async-start | bytes 7077888 | tf_op jit(solution)/shard_map/reduce_scatter | solution.py:79
  290.8 10.1 %copy-start.9 = (f32[2,16,40,768]{3,2,1,0:T(8,128)S(1)}, f32[2,16,40,768]{3,2,1,0:T(8,128)}, u32[]{:S(2)}) copy-start(f32[2,16,40,768]{3,2,1,0:T(8,128)} %copy-done.8) | copy-start | bytes 11796484
  299.0 1.9 copy-start.10
  310.8 209.4 %reduce-scatter.4.cloned.1.call-start = ((), (), s32[]{:S(2)}) async-start(), calls=%async_computation.7 | async-start | bytes 7077888 | tf_op jit(solution)/shard_map/reduce_scatter | solution.py:79
  323.1 200.1 %copy-start.1 = (bf16[2048,32]{0,1:T(8,128)(2,1)S(1)}, bf16[2048,32]{0,1:T(8,128)(2,1)}, u32[]{:S(2)}) copy-start(bf16[2048,32]{0,1:T(8,128)(2,1)} %param.15) | copy-start | bytes 393220
Sparse Core Ops, SparseCore 0:
  216.3 236.3 all-reduce.2
Sparse Core Ops, SparseCore 1:
  290.6 81.2 reduce-scatter.7
  374.2 71.8 reduce-scatter.5
  448.3 71.9 reduce-scatter.3
where the time goes:
time: 531 us
  waiting for transfers between devices  321 us (60%)
  matrix products  82.8 us (16%)
  blocking collectives  71.2 us (13%)
  starting transfers between devices  20.8 us (4%)
  local copies, waits for them, and re-layouts  16.6 us (3%)
  between operations  15.9 us (3%)
    psum x1, waiting for transfers between devices, body(): lax.psum(jnp.concatenate([router_part, loss_rows], axis=0), ('dp', 'exper...  130 us
    all_to_all x1, blocking collectives, body(): lax.all_to_all(outgoing.reshape(expert_count, 1, slot_count, model_width)...  71.2 us
    all_to_all x1, waiting for transfers between devices, body(): lax.all_to_all(sending.reshape(expert_count, 1, slot_count, model_width),...  68.4 us
    all_to_all x1, waiting for transfers between devices, body(): lax.all_to_all(result, 'expert', split_axis=1, concat_axis=0, tiled=True)  64.9 us
    reduce_scatter x3, waiting for transfers between devices, reduced(): lax.psum_scatter(part.astype(BF), 'dp', scatter_dimension=0, tiled=True)  58.3 us
    dot_general x3, matrix products, reduced(): part = jnp.einsum('jsrd,jsrf->djf', left, right, preferred_element_type=F32)  32 us
    all_to_all x1, starting transfers between devices, body(): lax.all_to_all(sending.reshape(expert_count, 1, slot_count, model_width),...  14.7 us
    unnamed x29, local copies, waits for them, and re-layouts  11.1 us
  transfers between devices with their start and end apart: 6, of which 4 were waited for; matrix products, arithmetic and copies ran while one was open for 10% of the time, Pallas kernels for 0%

commit v1 on v0

--- a/solution.py
+++ b/solution.py
@@ -65,7 +65,7 @@
     )
     router_part = router_part[:, :expert_count] + router_part[:, expert_count:]
     loss_rows = jnp.zeros((8, expert_count), F32).at[0, :domain_count].set(local_loss)
-    summed = lax.psum(jnp.concatenate([router_part, loss_rows], axis=0), ("dp", "expert"))
+    summed = lax.psum(lax.psum(jnp.concatenate([router_part, loss_rows], axis=0), "dp"), "expert")
     back_grad = lax.all_to_all(
         sending.reshape(expert_count, 1, slot_count, model_width),
         "expert",

time: 531 us -> 658 us (1.24)
  waiting for transfers between devices: 321 us -> 450 us
    reduce_scatter x3, waiting for transfers between devices: 58.3 us -> 217 us  [reduced(): lax.psum_scatter(part.astype(BF), 'dp', scatter_dimension=0, tiled=True)]
    all_to_all x1, waiting for transfers between devices: 68.4 us -> 0.01 us  [body(): lax.all_to_all(sending.reshape(expert_count, 1, slot_count, model_width),...]
    psum x1 -> x2, waiting for transfers between devices: 130 us -> 168 us  [the longest x1 94.8 us: body(): lax.psum(lax.psum(jnp.concatenate([router_part, loss_rows], axis=0), 'dp'...]
  transfers between devices with their start and end apart: 6 -> 7, of which waited for: 4 -> 6; matrix products, arithmetic and copies ran while one was open for 10% -> 8% of each run, Pallas kernels for 0% -> 0%
where the time goes in v1:
time: 658 us; the launch traced here: 657 us
  waiting for transfers between devices  450 us (68%)
  matrix products  82.8 us (13%)
  blocking collectives  71.2 us (11%)
  starting transfers between devices  20.8 us (3%)
  local copies, waits for them, and re-layouts  16.5 us (3%)
  between operations  14 us (2%)
    reduce_scatter x3, waiting for transfers between devices, reduced(): lax.psum_scatter(part.astype(BF), 'dp', scatter_dimension=0, tiled=True)  217 us
    psum x1, waiting for transfers between devices, body(): lax.psum(lax.psum(jnp.concatenate([router_part, loss_rows], axis=0), 'dp'...  94.8 us
    psum x1, waiting for transfers between devices, body(): lax.psum(jnp.concatenate([router_part, loss_rows], axis=0), 'dp')  73.4 us
    all_to_all x1, blocking collectives, body(): lax.all_to_all(outgoing.reshape(expert_count, 1, slot_count, model_width)...  71.2 us
    all_to_all x1, waiting for transfers between devices, body(): lax.all_to_all(result, 'expert', split_axis=1, concat_axis=0, tiled=True)  64.9 us
    dot_general x3, matrix products, reduced(): part = jnp.einsum('jsrd,jsrf->djf', left, right, preferred_element_type=F32)  32 us
    all_to_all x1, starting transfers between devices, body(): lax.all_to_all(sending.reshape(expert_count, 1, slot_count, model_width),...  14.7 us
  transfers between devices with their start and end apart: 7, of which 6 were waited for; matrix products, arithmetic and copies ran while one was open for 8% of the time, Pallas kernels for 0%

profile of v1, /device:TPU:1, one launch (start us, length us, event | category | flops | bytes accessed | tf_op | source)
XLA Modules:
  0.0 657.3 jit_solution(14622293042635914174)
XLA Ops:
  8.0 4.9 convolution_convert_fusion
  13.0 71.2 %all_to_all.51 = bf16[32,1,40,2048]{3,2,1,0:T(8,128)(2,1)S(1)} all-to-all(bf16[32,1,40,2048]{3,2,1,0:T(8,128)(2,1)S(1)} %bitcast.69), channel_id=1, replica_groups=mesh['dp'=8,'expert'=16] {'expert'}, dimensions={0} | all-to-all | bytes 10485760 | tf_op jit(solution)/shard_map/all_to_all | solution.py:24
  84.2 4.4 fusion.5
  88.6 6.5 multiply_convert_fusion.4
  95.1 7.7 %fusion.19 = bf16[2,16,40,2048]{3,2,1,0:T(8,128)(2,1)S(1)} fusion(bf16[2,16,40,768]{3,2,1,0:T(8,128)(2,1)} %get-tuple-element.43, bf16[2048,2,768,1]{2,1,0,3:T(2,128)(2,1)} %bitcast.80), kind=kOutput, calls=%fused_computation.28 | convolution fusion | flops 4029153280 | bytes 13500416 | tf_op jit(solution)/shard_map/jsrf,djf->jsrd/dot_general | solution.py:36
  102.8 2.8 copy.51
  105.6 5.7 all-to-all-start.1
  111.4 4.3 fusion.38
  115.7 64.9 %all-to-all-done.1 = bf16[2,16,40,2048]{3,2,0,1:T(8,128)(2,1)} async-done(((bf16[2,16,40,2048]{3,2,0,1:T(8,128)(2,1)}), bf16[2,16,40,2048]{3,2,0,1:T(8,128)(2,1)}, u32[]{:S(2)}, u32[]{:S(2)}) %all-to-all-start.1) | async-done | bytes 5242912 | tf_op jit(solution)/shard_map/all_to_all | solution.py:37
  180.6 6.5 multiply_reduce_fusion.1
  187.3 7.4 %multiply_convert_fusion = (bf16[1280,2048]{1,0:T(8,128)(2,1)}, f32[1280]{0:T(1024)S(1)}) fusion(f32[1280]{0:T(1024)S(1)} %get-tuple-element.41, bf16[2,16,40,2048]{3,2,0,1:T(8,128)(2,1)} %all-to-all-done.1, f32[512,2048]{1,0:T(8,128)S(1)} %get-tuple-element.46, f32[512]{0:T(512)S(1)} %broadcast_multiply_fusion, s32[1280]{0:T(1024)S(1)} %eq.64), kind=kOutput, calls=%fused_computation.3 | convolution fusion | flops 2700212992 | bytes 14697472 | tf_op jit(solution)/shard_map/dot_general | solution.py:50
  194.6 14.7 %all-to-all-start.2 = ((bf16[32,1,40,2048]{3,2,1,0:T(8,128)(2,1)}), bf16[32,1,40,2048]{3,2,1,0:T(8,128)(2,1)}, u32[]{:S(2)}, u32[]{:S(2)}) async-start(bf16[32,1,40,2048]{3,2,1,0:T(8,128)(2,1)} %bitcast.74), calls=%async_computation.2 | async-start | bytes 10485760 | tf_op jit(solution)/shard_map/all_to_all | solution.py:69
  211.4 73.4 %all-reduce.4.cloned.1.call-done = f32[2056,32]{0,1:T(8,128)} async-done(((f32[2056,32]{0,1:T(8,128)}), f32[2056,32]{0,1:T(8,128)}) %all-reduce.4.cloned.1.call-update) | async-done | bytes 263184 | tf_op jit(solution)/shard_map/psum | solution.py:68
  284.9 9.8 %fusion.2 = bf16[2048,2,768]{0,2,1:T(8,128)(2,1)} fusion(bf16[2,16,40,768]{3,2,1,0:T(8,128)(2,1)} %get-tuple-element.43, bf16[16,2,1,40,2048]{4,3,1,0,2:T(8,128)(2,1)} %bitcast.18), kind=kOutput, calls=%fused_computation.8 | convolution fusion | flops 4029677568 | bytes 13500416 | tf_op jit(solution)/shard_map/jsrd,jsrf->djf/dot_general | solution.py:78
  295.0 8.2 %fusion.7 = f32[2,16,40,768]{3,2,1,0:T(8,128)S(1)} fusion(bf16[2048,2,768,1]{2,1,0,3:T(2,128)(2,1)} %bitcast.81, bf16[16,2,1,40,2048]{4,3,1,0,2:T(8,128)(2,1)} %bitcast.18), kind=kOutput, calls=%fused_computation.13 | convolution fusion | flops 4026531840 | bytes 15466496 | tf_op jit(solution)/shard_map/jsrd,djf->jsrf/dot_general | solution.py:82
  305.1 9.9 %fusion.1 = bf16[2048,2,768]{0,2,1:T(8,128)(2,1)} fusion(bf16[16,2,1,40,2048]{4,3,1,0,2:T(8,128)(2,1)} %bitcast.72, f32[2,16,40,768]{3,2,1,0:T(8,128)S(1)} %fusion.7, f32[2,16,40,768]{3,2,1,0:T(8,128)S(1)} %copy-done.9), kind=kOutput, calls=%fused_computation.7 | convolution fusion | flops 4035575808 | bytes 19398656 | tf_op jit(solution)/shard_map/jsrd,jsrf->djf/dot_general | solution.py:78
  315.0 12.3 %fusion = bf16[2048,2,768]{0,2,1:T(8,128)(2,1)} fusion(bf16[16,2,1,40,2048]{4,3,1,0,2:T(8,128)(2,1)} %bitcast.73, f32[2,16,40,768]{3,2,1,0:T(8,128)} %copy-done.8, f32[2,16,40,768]{3,2,1,0:T(8,128)} %copy-done.10, f32[2,16,40,768]{3,2,1,0:T(8,128)} %get-tuple-element.44), kind=kOutput, calls=%fused_computation.6 | convolution fusion | flops 4039507968 | bytes 23330816 | tf_op jit(solution)/shard_map/jsrd,jsrf->djf/dot_general | solution.py:78
  327.3 94.8 %all-reduce.6.cloned.1.call-done = f32[2056,32]{0,1:T(8,128)} async-done(((f32[2056,32]{0,1:T(8,128)}), f32[2056,32]{0,1:T(8,128)}) %all-reduce.6.cloned.1.call-update) | async-done | bytes 263184 | tf_op jit(solution)/shard_map/psum | solution.py:68
  425.1 74.6 %reduce-scatter.8.cloned.1.call-done = bf16[256,2,768]{0,2,1:T(8,128)(2,1)} async-done(((bf16[2048,2,768]{0,2,1:T(8,128)(2,1)}), bf16[256,2,768]{0,2,1:T(8,128)(2,1)}) %reduce-scatter.8.cloned.1.call-update) | async-done | bytes 786448 | tf_op jit(solution)/shard_map/reduce_scatter | solution.py:79
  499.7 3.0 copy.58
  502.8 71.0 %reduce-scatter.6.cloned.1.call-done = bf16[256,2,768]{0,2,1:T(8,128)(2,1)} async-done(((bf16[2048,2,768]{0,2,1:T(8,128)(2,1)}), bf16[256,2,768]{0,2,1:T(8,128)(2,1)}) %reduce-scatter.6.cloned.1.call-update) | async-done | bytes 786448 | tf_op jit(solution)/shard_map/reduce_scatter | solution.py:79
  573.7 3.0 copy.57
  576.8 70.9 %reduce-scatter.4.cloned.1.call-done = bf16[256,2,768]{0,2,1:T(8,128)(2,1)} async-done(((bf16[2048,2,768]{0,2,1:T(8,128)(2,1)}), bf16[256,2,768]{0,2,1:T(8,128)(2,1)}) %reduce-scatter.4.cloned.1.call-update) | async-done | bytes 786448 | tf_op jit(solution)/shard_map/reduce_scatter | solution.py:79
  647.7 3.0 copy.56
  (53 shorter events, 8.4 us)
Async XLA Ops:
  7.2 104.2 %copy-start = (bf16[2048,32]{0,1:T(8,128)(2,1)S(1)}, bf16[2048,32]{0,1:T(8,128)(2,1)}, u32[]{:S(2)}) copy-start(bf16[2048,32]{0,1:T(8,128)(2,1)} %param.15) | copy-start | bytes 393220
  12.9 71.2 %copy-start.2 = (bf16[1280,2048]{1,0:T(8,128)(2,1)}, bf16[1280,2048]{1,0:T(8,128)(2,1)S(1)}, u32[]{:S(2)}) copy-start(bf16[1280,2048]{1,0:T(8,128)(2,1)S(1)} %convolution_convert_fusion) | copy-start | bytes 15728644
  13.0 71.2 %copy-start.7 = (bf16[2048,2,768]{2,1,0:T(2,128)(2,1)S(1)}, bf16[2048,2,768]{2,1,0:T(2,128)(2,1)}, u32[]{:S(2)}) copy-start(bf16[2048,2,768]{2,1,0:T(2,128)(2,1)} %param.17) | copy-start | bytes 18874372
  13.0 75.6 %slice-start = ((s8[6291456]{0:T(1024)(128)(4,1)}), s8[4194304]{0:T(1024)(128)(4,1)S(1)}, s32[]{:S(2)}) async-start(s8[6291456]{0:T(1024)(128)(4,1)} %bitcast.77), calls=%async_computation.11 | async-start | bytes 8388608
  84.2 4.4 copy-start.3
  84.2 4.4 slice-start.1
  88.6 6.6 copy-start.8
  105.6 75.0 %all-to-all-start.1 = ((bf16[2,16,40,2048]{3,2,0,1:T(8,128)(2,1)}), bf16[2,16,40,2048]{3,2,0,1:T(8,128)(2,1)}, u32[]{:S(2)}, u32[]{:S(2)}) async-start(bf16[2,16,40,2048]{3,2,0,1:T(8,128)(2,1)} %copy.51), calls=%async_computation.1 | async-start | bytes 10485760 | tf_op jit(solution)/shard_map/all_to_all | solution.py:37
  111.3 69.3 %copy-start.4 = (bf16[512,2048]{1,0:T(8,128)(2,1)S(1)}, bf16[512,2048]{1,0:T(8,128)(2,1)}, u32[]{:S(2)}) copy-start(bf16[512,2048]{1,0:T(8,128)(2,1)} %param.11) | copy-start | bytes 6291460
  180.6 6.5 copy-start.5
  180.6 6.5 copy-start.6
  194.6 90.3 %all-to-all-start.2 = ((bf16[32,1,40,2048]{3,2,1,0:T(8,128)(2,1)}), bf16[32,1,40,2048]{3,2,1,0:T(8,128)(2,1)}, u32[]{:S(2)}, u32[]{:S(2)}) async-start(bf16[32,1,40,2048]{3,2,1,0:T(8,128)(2,1)} %bitcast.74), calls=%async_computation.2 | async-start | bytes 10485760 | tf_op jit(solution)/shard_map/all_to_all | solution.py:69
  209.3 75.5 %all-reduce.4.cloned.1.call-start = ((), (), s32[]{:S(2)}) async-start(), calls=%async_computation.6 | async-start | bytes 557056 | tf_op jit(solution)/shard_map/psum | solution.py:68
  211.4 210.7 %all-reduce.6.cloned.1.call-start = ((), (), s32[]{:S(2)}) async-start(), calls=%async_computation.7 | async-start | bytes 557056 | tf_op jit(solution)/shard_map/psum | solution.py:68
  284.8 214.9 %reduce-scatter.8.cloned.1.call-start = ((), (), s32[]{:S(2)}) async-start(), calls=%async_computation.10 | async-start | bytes 7077888 | tf_op jit(solution)/shard_map/reduce_scatter | solution.py:79
  294.7 279.0 %reduce-scatter.6.cloned.1.call-start = ((), (), s32[]{:S(2)}) async-start(), calls=%async_computation.9 | async-start | bytes 7077888 | tf_op jit(solution)/shard_map/reduce_scatter | solution.py:79
  295.0 10.1 %copy-start.9 = (f32[2,16,40,768]{3,2,1,0:T(8,128)S(1)}, f32[2,16,40,768]{3,2,1,0:T(8,128)}, u32[]{:S(2)}) copy-start(f32[2,16,40,768]{3,2,1,0:T(8,128)} %copy-done.8) | copy-start | bytes 11796484
  303.2 1.9 copy-start.10
  315.0 332.7 %reduce-scatter.4.cloned.1.call-start = ((), (), s32[]{:S(2)}) async-start(), calls=%async_computation.8 | async-start | bytes 7077888 | tf_op jit(solution)/shard_map/reduce_scatter | solution.py:79
  327.3 323.4 %copy-start.1 = (bf16[2048,32]{0,1:T(8,128)(2,1)S(1)}, bf16[2048,32]{0,1:T(8,128)(2,1)}, u32[]{:S(2)}) copy-start(bf16[2048,32]{0,1:T(8,128)(2,1)} %param.15) | copy-start | bytes 393220
Sparse Core Ops, SparseCore 0:
  213.2 71.5 all-reduce.3
  287.5 134.6 all-reduce.5
  424.5 75.1 reduce-scatter.7
  502.0 71.6 reduce-scatter.5
  576.0 71.6 reduce-scatter.3
